TPU v7x, 32 devices: a whole 2x2x4 slice. The times are simulated.
32 devices in a mesh: lat: 4 (over x, core), lon: 8 (over z, y).
Axes of the slice: x: 2, y: 2, z: 4, core: 2. Of those that a mesh axis runs over, the one named last changes fastest.
Arguments:
- queries: bfloat16 [8192, 2048], P(('lat', 'lon')), may hold values from -340 to 340
- keys: bfloat16 [8192, 2048], P(('lat', 'lon')), may hold values from -12 to 12
- values: bfloat16 [8192, 2048], P(('lat', 'lon')), may hold values from -6 to 6
- partners: int32 [32, 5], P(('lat', 'lon')), may hold values from -1 to 31, as said below
- out_weight: bfloat16 [2048, 2048], P(None, 'lat'), may hold values from -0.125 to 0.125
Outputs:
- projected: bfloat16 [8192, 2048], P(('lat', 'lon'))
Inputs may be any that keep to these rules, and one draw needn't show every extreme that they name: `partners`: for each block, the first entries of its row are distinct blocks of its own band, none in its own sector or the two sectors beside it; the remaining entries are -1. In every band some block uses all 5 slots.
All inputs are finite; a program needn't handle non-finite values.
Results may differ from a plain program's by a relative error of at most 0.0095.
Values may be sent and summed in bfloat16 or wider, within the bound.
No kernel may reach another device: no remote copies, remote signals or barrier semaphores. Data moves between devices by JAX's collectives and lax.ppermute only.
A program may use at most 128 MiB of HBM per device.

v0:
```python
import math
import jax
import jax.numpy as jnp
from jax import lax
from jax.sharding import PartitionSpec as P

HEADS = 16
HEAD_DIM = 128
very_low = -1e30


def membership(listed_row, sector, band_start, sectors, lon_count):
    nearby = (
        (sectors == sector)
        | (sectors == (sector + 1) % lon_count)
        | (sectors == (sector + lon_count - 1) % lon_count)
    )
    named = jnp.any(listed_row[:, None] - band_start == sectors[None, :], axis=0)
    return nearby | named


def per_device(queries, keys, values, partners, out_weight):
    lon_count = lax.axis_size("lon")
    band_start = lax.axis_index("lat") * lon_count
    score_scale = 1.0 / math.sqrt(HEAD_DIM)
    sectors = jnp.arange(lon_count, dtype=jnp.int32)
    block_rows = queries.shape[0]
    local_heads = HEADS // lon_count
    q_all, k_all, v_all = (
        lax.all_to_all(queries[None], "lon", split_axis=2, concat_axis=0, tiled=True),
        lax.all_to_all(keys[None], "lon", split_axis=2, concat_axis=0, tiled=True),
        lax.all_to_all(values[None], "lon", split_axis=2, concat_axis=0, tiled=True),
    )
    all_lists = lax.all_gather(partners, "lon", axis=0, tiled=True)
    key_flat = k_all.reshape(lon_count * block_rows, local_heads, HEAD_DIM)
    value_flat = v_all.reshape(lon_count * block_rows, local_heads, HEAD_DIM)

    def one_query(element):
        query_block, listed_row, position = element
        member = membership(listed_row, position, band_start, sectors, lon_count)
        key_mask = jnp.repeat(member, block_rows, total_repeat_length=lon_count * block_rows)
        query_heads = query_block.reshape(block_rows, local_heads, HEAD_DIM)
        scores = (
            jnp.einsum("qhd,khd->hqk", query_heads, key_flat, preferred_element_type=jnp.float32)
            * score_scale
        )
        scores = jnp.where(key_mask[None, None, :], scores, very_low)
        row_max = jnp.max(scores, axis=-1, keepdims=True)
        weights = jnp.exp(scores - row_max)
        row_total = jnp.sum(weights, axis=-1)
        mixture = jnp.einsum(
            "hqk,khd->qhd",
            weights.astype(jnp.bfloat16),
            value_flat,
            preferred_element_type=jnp.float32,
        )
        attended_heads = mixture / row_total.T[:, :, None]
        return attended_heads.reshape(block_rows, local_heads * HEAD_DIM).astype(jnp.bfloat16)

    per_block = lax.map(one_query, (q_all, all_lists, sectors))
    returned = lax.all_to_all(per_block, "lon", split_axis=0, concat_axis=2, tiled=True)
    attended = returned[0]
    projected = jnp.dot(
        attended,
        lax.all_gather(out_weight, "lat", axis=1, tiled=True),
        preferred_element_type=jnp.float32,
    )
    return projected.astype(jnp.bfloat16)


def solution(mesh):
    return jax.shard_map(
        per_device,
        mesh=mesh,
        in_specs=(
            P(("lat", "lon"), None),
            P(("lat", "lon"), None),
            P(("lat", "lon"), None),
            P(("lat", "lon"), None),
            P(None, "lat"),
        ),
        out_specs=P(("lat", "lon"), None),
        check_vma=False,
    )
```

profile of v0, /device:TPU:0, one launch (start us, length us, event | category | flops | bytes accessed | tf_op | source)
XLA Modules:
  0.0 282.5 jit_solution(2650263605104640194)
XLA Ops:
  6.5 4.6 %copy.34 = bf16[1,256,2048]{1,0,2:T(2,128)(2,1)S(1)} copy(bf16[1,256,2048]{2,1,0:T(8,128)(2,1)} %bitcast.106) | data formatting | bytes 2097152 | tf_op jit(solution)/shard_map/broadcast_in_dim | solution.py:31
  11.7 10.6 %reduce.3 = bf16[2048,256]{1,0:T(8,128)(2,1)S(1)} reduce(bf16[2048,1,256]{2,1,0:T(2,128)(2,1)S(1)} %bitcast.98, bf16[]{:T(256)} %broadcast.279), dimensions={1}, to_apply=%bitcast.51.reduce_sub_computation | reduce | bytes 2097154
  22.3 1.1 reshape.254
  23.4 7.3 %all-to-all-start.1 = ((bf16[8,2,32768]{2,1,0:T(2,128)(2,1)}), bf16[8,2,32768]{2,1,0:T(2,128)(2,1)S(1)}, u32[]{:S(2)}, u32[]{:S(2)}) async-start(bf16[8,2,32768]{2,1,0:T(2,128)(2,1)} %reshape.254), calls=%async_computation.1 | async-start | bytes 2097152 | tf_op jit(solution)/shard_map/all_to_all | solution.py:31
  30.7 4.6 %copy.36 = bf16[1,256,2048]{1,0,2:T(2,128)(2,1)S(1)} copy(bf16[1,256,2048]{2,1,0:T(8,128)(2,1)} %bitcast.107) | data formatting | bytes 2097152 | tf_op jit(solution)/shard_map/broadcast_in_dim | solution.py:32
  35.3 11.6 %reduce.4 = bf16[2048,256]{1,0:T(8,128)(2,1)} reduce(bf16[2048,1,256]{2,1,0:T(2,128)(2,1)S(1)} %bitcast.100, bf16[]{:T(256)} %broadcast.279), dimensions={1}, to_apply=%bitcast.53.reduce_sub_computation | reduce | bytes 2097154
  46.9 2.1 reshape.256
  49.0 7.4 %all-to-all-done.1 = bf16[8,2,32768]{2,1,0:T(2,128)(2,1)S(1)} async-done(((bf16[8,2,32768]{2,1,0:T(2,128)(2,1)}), bf16[8,2,32768]{2,1,0:T(2,128)(2,1)S(1)}, u32[]{:S(2)}, u32[]{:S(2)}) %all-to-all-start.1) | async-done | bytes 1048608 | tf_op jit(solution)/shard_map/all_to_all | solution.py:31
  56.5 4.2 %all-to-all-start.2 = ((bf16[8,2,32768]{2,1,0:T(2,128)(2,1)}), bf16[8,2,32768]{2,1,0:T(2,128)(2,1)}, u32[]{:S(2)}, u32[]{:S(2)}) async-start(bf16[8,2,32768]{2,1,0:T(2,128)(2,1)} %reshape.256), calls=%async_computation.2 | async-start | bytes 2097152 | tf_op jit(solution)/shard_map/all_to_all | solution.py:32
  60.7 4.6 %copy.33 = bf16[1,256,2048]{1,0,2:T(2,128)(2,1)S(1)} copy(bf16[1,256,2048]{2,1,0:T(8,128)(2,1)} %bitcast.108) | data formatting | bytes 2097152 | tf_op jit(solution)/shard_map/broadcast_in_dim | solution.py:30
  65.3 11.6 %reduce.2 = bf16[2048,256]{1,0:T(8,128)(2,1)} reduce(bf16[2048,1,256]{2,1,0:T(2,128)(2,1)S(1)} %bitcast.99, bf16[]{:T(256)} %broadcast.279), dimensions={1}, to_apply=%bitcast.49.reduce_sub_computation | reduce | bytes 2097154
  76.9 2.1 reshape.252
  79.0 7.3 %all-to-all-done.2 = bf16[8,2,32768]{2,1,0:T(2,128)(2,1)} async-done(((bf16[8,2,32768]{2,1,0:T(2,128)(2,1)}), bf16[8,2,32768]{2,1,0:T(2,128)(2,1)}, u32[]{:S(2)}, u32[]{:S(2)}) %all-to-all-start.2) | async-done | bytes 1048608 | tf_op jit(solution)/shard_map/all_to_all | solution.py:32
  86.3 4.2 %all-to-all-start = ((bf16[8,2,32768]{2,1,0:T(2,128)(2,1)}), bf16[8,2,32768]{2,1,0:T(2,128)(2,1)}, u32[]{:S(2)}, u32[]{:S(2)}) async-start(bf16[8,2,32768]{2,1,0:T(2,128)(2,1)} %reshape.252), calls=%async_computation | async-start | bytes 2097152 | tf_op jit(solution)/shard_map/all_to_all | solution.py:30
  91.3 30.1 %all-gather = s32[8,1,5]{2,1,0:T(1,128)S(1)} all-gather(s32[1,1,5]{2,1,0:T(1,128)S(1)} %bitcast.111), channel_id=1, replica_groups=mesh['lat'=4,'lon'=8] {'lon'}, dimensions={0}, use_global_device_ids=true | all-gather | bytes 180 | tf_op jit(solution)/shard_map/all_gather | solution.py:34
  121.4 1.0 reshape.255
  124.5 4.3 %reshape.257 = bf16[2048,1,256]{2,1,0:T(2,128)(2,1)S(1)} reshape(bf16[8,2,32768]{2,1,0:T(2,128)(2,1)} %all-to-all-done.2) | data formatting | bytes 2097152
  129.6 1.4 reshape.233
  131.0 4.3 %reshape.253 = bf16[2048,1,256]{2,1,0:T(2,128)(2,1)S(1)} reshape(bf16[8,2,32768]{2,1,0:T(2,128)(2,1)} %all-to-all-done) | data formatting | bytes 2097152
  135.3 1.1 copy.40
  136.5 102.6 %while.18 = (s32[]{:T(128)}, bf16[8,256,256]{1,2,0:T(8,128)(2,1)}, s32[8]{0:T(128)S(1)}, s32[8,5]{1,0:T(8,128)S(1)}, s32[]{:T(128)}, /*index=5*/bf16[8,256,256]{...) while((s32[]{:T(128)}, bf16[8,256,256]{1,2,0:T(8,128)(2,1)}, ...), condition=%wide.region_4.5_spmd.clone, body=%wide.region_0.4_spmd.clone.sunk | while | flops 548549760 | bytes 19694732 | solution.py:60
  139.9 4.9 %select_select_fusion.2 = pred[2048]{0:T(1024)(128)(4,1)S(1)} fusion(pred[2048]{0:T(1024)(128)(4,1)S(1)} %get-tuple-element.493, pred[2048]{0:T(1024)(128)(4,1)S(1)} %get-tuple-element.494, pred[2048]{0:T(1024)(128)(4,1)S(1)} %get-tuple-element.495, pred[2048]{0:T(1024)(128)(4,1)S(1)} %get-tuple-element.496, ...), kind=kLoop, calls=%fused_computation.10.clone.1 | loop fusion | flops 14336 | bytes 16392 | tf_op jit(solution)/shard_map/while/body/eval_jaxpr/jit(_take)/gather | solution.py:41
  146.6 0.9 fusion.41
  147.5 1.1 fusion.42
  152.7 4.9 %select_select_fusion.2 = pred[2048]{0:T(1024)(128)(4,1)S(1)} fusion(pred[2048]{0:T(1024)(128)(4,1)S(1)} %get-tuple-element.493, pred[2048]{0:T(1024)(128)(4,1)S(1)} %get-tuple-element.494, pred[2048]{0:T(1024)(128)(4,1)S(1)} %get-tuple-element.495, pred[2048]{0:T(1024)(128)(4,1)S(1)} %get-tuple-element.496, ...), kind=kLoop, calls=%fused_computation.10.clone.1 | loop fusion | flops 14336 | bytes 16392 | tf_op jit(solution)/shard_map/while/body/eval_jaxpr/jit(_take)/gather | solution.py:41
  158.5 0.9 fusion.40
  159.4 0.9 fusion.41
  160.4 1.1 fusion.42
  165.5 4.9 %select_select_fusion.2 = pred[2048]{0:T(1024)(128)(4,1)S(1)} fusion(pred[2048]{0:T(1024)(128)(4,1)S(1)} %get-tuple-element.493, pred[2048]{0:T(1024)(128)(4,1)S(1)} %get-tuple-element.494, pred[2048]{0:T(1024)(128)(4,1)S(1)} %get-tuple-element.495, pred[2048]{0:T(1024)(128)(4,1)S(1)} %get-tuple-element.496, ...), kind=kLoop, calls=%fused_computation.10.clone.1 | loop fusion | flops 14336 | bytes 16392 | tf_op jit(solution)/shard_map/while/body/eval_jaxpr/jit(_take)/gather | solution.py:41
  172.2 0.9 fusion.41
  173.2 1.1 fusion.42
  178.3 4.9 %select_select_fusion.2 = pred[2048]{0:T(1024)(128)(4,1)S(1)} fusion(pred[2048]{0:T(1024)(128)(4,1)S(1)} %get-tuple-element.493, pred[2048]{0:T(1024)(128)(4,1)S(1)} %get-tuple-element.494, pred[2048]{0:T(1024)(128)(4,1)S(1)} %get-tuple-element.495, pred[2048]{0:T(1024)(128)(4,1)S(1)} %get-tuple-element.496, ...), kind=kLoop, calls=%fused_computation.10.clone.1 | loop fusion | flops 14336 | bytes 16392 | tf_op jit(solution)/shard_map/while/body/eval_jaxpr/jit(_take)/gather | solution.py:41
  185.0 0.9 fusion.41
  186.0 1.1 fusion.42
  191.1 4.9 %select_select_fusion.2 = pred[2048]{0:T(1024)(128)(4,1)S(1)} fusion(pred[2048]{0:T(1024)(128)(4,1)S(1)} %get-tuple-element.493, pred[2048]{0:T(1024)(128)(4,1)S(1)} %get-tuple-element.494, pred[2048]{0:T(1024)(128)(4,1)S(1)} %get-tuple-element.495, pred[2048]{0:T(1024)(128)(4,1)S(1)} %get-tuple-element.496, ...), kind=kLoop, calls=%fused_computation.10.clone.1 | loop fusion | flops 14336 | bytes 16392 | tf_op jit(solution)/shard_map/while/body/eval_jaxpr/jit(_take)/gather | solution.py:41
  197.9 0.9 fusion.41
  198.8 1.1 fusion.42
  204.0 4.9 %select_select_fusion.2 = pred[2048]{0:T(1024)(128)(4,1)S(1)} fusion(pred[2048]{0:T(1024)(128)(4,1)S(1)} %get-tuple-element.493, pred[2048]{0:T(1024)(128)(4,1)S(1)} %get-tuple-element.494, pred[2048]{0:T(1024)(128)(4,1)S(1)} %get-tuple-element.495, pred[2048]{0:T(1024)(128)(4,1)S(1)} %get-tuple-element.496, ...), kind=kLoop, calls=%fused_computation.10.clone.1 | loop fusion | flops 14336 | bytes 16392 | tf_op jit(solution)/shard_map/while/body/eval_jaxpr/jit(_take)/gather | solution.py:41
  210.7 0.9 fusion.41
  211.6 1.1 fusion.42
  216.8 4.9 %select_select_fusion.2 = pred[2048]{0:T(1024)(128)(4,1)S(1)} fusion(pred[2048]{0:T(1024)(128)(4,1)S(1)} %get-tuple-element.493, pred[2048]{0:T(1024)(128)(4,1)S(1)} %get-tuple-element.494, pred[2048]{0:T(1024)(128)(4,1)S(1)} %get-tuple-element.495, pred[2048]{0:T(1024)(128)(4,1)S(1)} %get-tuple-element.496, ...), kind=kLoop, calls=%fused_computation.10.clone.1 | loop fusion | flops 14336 | bytes 16392 | tf_op jit(solution)/shard_map/while/body/eval_jaxpr/jit(_take)/gather | solution.py:41
  223.5 0.9 fusion.41
  224.5 1.1 fusion.42
  229.6 4.9 %select_select_fusion.2 = pred[2048]{0:T(1024)(128)(4,1)S(1)} fusion(pred[2048]{0:T(1024)(128)(4,1)S(1)} %get-tuple-element.493, pred[2048]{0:T(1024)(128)(4,1)S(1)} %get-tuple-element.494, pred[2048]{0:T(1024)(128)(4,1)S(1)} %get-tuple-element.495, pred[2048]{0:T(1024)(128)(4,1)S(1)} %get-tuple-element.496, ...), kind=kLoop, calls=%fused_computation.10.clone.1 | loop fusion | flops 14336 | bytes 16392 | tf_op jit(solution)/shard_map/while/body/eval_jaxpr/jit(_take)/gather | solution.py:41
  236.3 0.9 fusion.41
  237.3 1.1 fusion.42
  239.1 29.9 %all_to_all.63 = bf16[8,256,256]{1,2,0:T(8,128)(2,1)S(1)} all-to-all(bf16[8,256,256]{1,2,0:T(8,128)(2,1)} %get-tuple-element.287), channel_id=1, replica_groups=mesh['lat'=4,'lon'=8] {'lon'}, dimensions={0} | all-to-all | bytes 2097152 | tf_op jit(solution)/shard_map/all_to_all | solution.py:61
  269.0 6.7 %convolution_convert_fusion = bf16[256,2048]{1,0:T(8,128)(2,1)} fusion(bf16[256,2048]{0,1:T(8,128)(2,1)S(1)} %bitcast.101, bf16[2048,2048]{1,0:T(8,128)(2,1)} %all-gather.3.cloned.1.call-done), kind=kOutput, calls=%fused_computation.20 | convolution fusion | flops 2148007936 | bytes 10485760 | tf_op jit(solution)/shard_map/dot_general | solution.py:63
  (108 shorter events, 39.5 us)
Async XLA Ops:
  23.4 33.1 %all-to-all-start.1 = ((bf16[8,2,32768]{2,1,0:T(2,128)(2,1)}), bf16[8,2,32768]{2,1,0:T(2,128)(2,1)S(1)}, u32[]{:S(2)}, u32[]{:S(2)}) async-start(bf16[8,2,32768]{2,1,0:T(2,128)(2,1)} %reshape.254), calls=%async_computation.1 | async-start | bytes 2097152 | tf_op jit(solution)/shard_map/all_to_all | solution.py:31
  56.5 29.8 %all-to-all-start.2 = ((bf16[8,2,32768]{2,1,0:T(2,128)(2,1)}), bf16[8,2,32768]{2,1,0:T(2,128)(2,1)}, u32[]{:S(2)}, u32[]{:S(2)}) async-start(bf16[8,2,32768]{2,1,0:T(2,128)(2,1)} %reshape.256), calls=%async_computation.2 | async-start | bytes 2097152 | tf_op jit(solution)/shard_map/all_to_all | solution.py:32
  65.3 26.0 %copy-start.8 = (s32[1,5]{1,0:T(1,128)S(1)}, s32[1,5]{1,0:T(1,128)}, u32[]{:S(2)}) copy-start(s32[1,5]{1,0:T(1,128)} %param.12) | copy-start | bytes 64
  86.3 44.7 %all-to-all-start = ((bf16[8,2,32768]{2,1,0:T(2,128)(2,1)}), bf16[8,2,32768]{2,1,0:T(2,128)(2,1)}, u32[]{:S(2)}, u32[]{:S(2)}) async-start(bf16[8,2,32768]{2,1,0:T(2,128)(2,1)} %reshape.252), calls=%async_computation | async-start | bytes 2097152 | tf_op jit(solution)/shard_map/all_to_all | solution.py:30
  90.5 178.4 %all-gather.3.cloned.1.call-start = ((), (), s32[]{:S(2)}) async-start(), calls=%async_computation.4 | async-start | bytes 10485760 | tf_op jit(solution)/shard_map/all_gather | solution.py:65
  129.6 6.9 %copy-start.1 = (pred[2048]{0:T(1024)(128)(4,1)S(1)}, pred[2048]{0:T(1024)(128)(4,1)}, u32[]{:S(2)}) copy-start(pred[2048]{0:T(1024)(128)(4,1)} %constant.324) | copy-start | bytes 6148
  129.6 6.9 %copy-start.2 = (pred[2048]{0:T(1024)(128)(4,1)S(1)}, pred[2048]{0:T(1024)(128)(4,1)}, u32[]{:S(2)}) copy-start(pred[2048]{0:T(1024)(128)(4,1)} %constant.325) | copy-start | bytes 6148
  129.6 6.9 %copy-start.3 = (pred[2048]{0:T(1024)(128)(4,1)S(1)}, pred[2048]{0:T(1024)(128)(4,1)}, u32[]{:S(2)}) copy-start(pred[2048]{0:T(1024)(128)(4,1)} %constant.326) | copy-start | bytes 6148
  129.6 6.9 %copy-start.4 = (pred[2048]{0:T(1024)(128)(4,1)S(1)}, pred[2048]{0:T(1024)(128)(4,1)}, u32[]{:S(2)}) copy-start(pred[2048]{0:T(1024)(128)(4,1)} %constant.327) | copy-start | bytes 6148
  129.6 6.9 %copy-start.5 = (pred[2048]{0:T(1024)(128)(4,1)S(1)}, pred[2048]{0:T(1024)(128)(4,1)}, u32[]{:S(2)}) copy-start(pred[2048]{0:T(1024)(128)(4,1)} %constant.328) | copy-start | bytes 6148
  129.6 6.9 %copy-start.6 = (pred[2048]{0:T(1024)(128)(4,1)S(1)}, pred[2048]{0:T(1024)(128)(4,1)}, u32[]{:S(2)}) copy-start(pred[2048]{0:T(1024)(128)(4,1)} %constant.329) | copy-start | bytes 6148
  129.6 6.9 %copy-start.7 = (pred[2048]{0:T(1024)(128)(4,1)S(1)}, pred[2048]{0:T(1024)(128)(4,1)}, u32[]{:S(2)}) copy-start(pred[2048]{0:T(1024)(128)(4,1)} %constant.330) | copy-start | bytes 6148
  145.7 1.9 copy-start
  158.5 1.9 copy-start
  171.3 1.9 copy-start
  184.1 1.9 copy-start
  196.9 1.9 copy-start
  209.8 1.9 copy-start
  222.6 1.9 copy-start
  235.4 1.9 copy-start
Sparse Core Ops, SparseCore 0:
  92.9 59.5 all-gather.2
where the time goes:
time: 284 us; the launch traced here: 283 us
  other arithmetic  86.1 us (30%)
  blocking collectives  60 us (21%)
  local copies, waits for them, and re-layouts  57.7 us (20%)
  matrix products  23.1 us (8%)
  starting transfers between devices  15.8 us (6%)
  waiting for transfers between devices  15.4 us (5%)
  between operations  13.6 us (5%)
  loops' own time  10.8 us (4%)
    gather x8, other arithmetic, one_query(): jnp.repeat(member, block_rows, total_repeat_length=lon_count * block_rows)  38.9 us
    unnamed x3, other arithmetic  33.7 us
    all_gather x1, blocking collectives, per_device(): all_lists = lax.all_gather(partners, 'lon', axis=0, tiled=True)  30.1 us
    all_to_all x1, blocking collectives, per_device(): lax.all_to_all(per_block, 'lon', split_axis=0, concat_axis=2, tiled=True)  29.9 us
    unnamed x27, local copies, waits for them, and re-layouts  17.8 us
    dynamic_slice x16, local copies, waits for them, and re-layouts, per_device(): per_block = lax.map(one_query, (q_all, all_lists, sectors))  12.2 us
    another operation x1, loops' own time, per_device(): per_block = lax.map(one_query, (q_all, all_lists, sectors))  10.8 us
    dot_general x8, matrix products, one_query(): jnp.einsum('hqk,khd->qhd', weights.astype(jnp.bfloat16), value_flat, pref...  9.01 us
  transfers between devices with their start and end apart: 4, of which 2 were waited for; matrix products, arithmetic and copies ran while one was open for 51% of the time, Pallas kernels for 0%

commit v1 on v0

--- a/solution.py
+++ b/solution.py
@@ -3,6 +3,7 @@
 import jax.numpy as jnp
 from jax import lax
 from jax.sharding import PartitionSpec as P
+from jax.lax import axis_index, ppermute, psum
 
 HEADS = 16
 HEAD_DIM = 128
@@ -31,7 +32,16 @@
         lax.all_to_all(keys[None], "lon", split_axis=2, concat_axis=0, tiled=True),
         lax.all_to_all(values[None], "lon", split_axis=2, concat_axis=0, tiled=True),
     )
-    all_lists = lax.all_gather(partners, "lon", axis=0, tiled=True)
+    n_lanes = psum(1, axis_name="lon")
+    next_value = sorted(((i, (i + 1) % n_lanes) for i in range(n_lanes)))
+    back = partners
+    ledger = [back]
+    for it in range(1, n_lanes):
+        back = ppermute(back, axis_name="lon", perm=next_value)
+        ledger.insert(0, back)
+    arr_out = jnp.concatenate(ledger, axis=0)
+    wide_out = axis_index("lon") + 1
+    all_lists = jnp.roll(arr_out, wide_out * partners.shape[0], axis=0)
     key_flat = k_all.reshape(lon_count * block_rows, local_heads, HEAD_DIM)
     value_flat = v_all.reshape(lon_count * block_rows, local_heads, HEAD_DIM)
 

time: 284 us -> 304 us (1.070)
  waiting for transfers between devices: 15.4 us -> 71.5 us
  blocking collectives: 60 us -> 21.1 us
    ppermute x0 -> x7, waiting for transfers between devices: none -> 56.9 us  [per_device(): back = ppermute(back, axis_name='lon', perm=next_value)]
    all_gather x1 -> x0, blocking collectives: 30.1 us -> none  [per_device(): all_lists = lax.all_gather(partners, 'lon', axis=0, tiled=True)]
    all_to_all x1, blocking collectives: 29.9 us -> 21.1 us  [per_device(): lax.all_to_all(per_block, 'lon', split_axis=0, concat_axis=2, tiled=True)]
  transfers between devices with their start and end apart: 4 -> 11, of which waited for: 2 -> 9; matrix products, arithmetic and copies ran while one was open for 51% -> 48% of each run, Pallas kernels for 0% -> 0%
where the time goes in v1:
time: 304 us; the launch traced here: 302 us
  other arithmetic  86.7 us (29%)
  waiting for transfers between devices  71.5 us (24%)
  local copies, waits for them, and re-layouts  57.7 us (19%)
  matrix products  23 us (8%)
  blocking collectives  21.1 us (7%)
  starting transfers between devices  17.8 us (6%)
  between operations  13.7 us (5%)
  loops' own time  10.6 us (3%)
    ppermute x7, waiting for transfers between devices, per_device(): back = ppermute(back, axis_name='lon', perm=next_value)  56.9 us
    gather x8, other arithmetic, one_query(): jnp.repeat(member, block_rows, total_repeat_length=lon_count * block_rows)  39.4 us
    unnamed x3, other arithmetic  33.9 us
    all_to_all x1, blocking collectives, per_device(): lax.all_to_all(per_block, 'lon', split_axis=0, concat_axis=2, tiled=True)  21.1 us
    unnamed x27, local copies, waits for them, and re-layouts  17.8 us
    dynamic_slice x16, local copies, waits for them, and re-layouts, per_device(): per_block = lax.map(one_query, (q_all, all_lists, sectors))  12.1 us
    another operation x1, loops' own time, per_device(): per_block = lax.map(one_query, (q_all, all_lists, sectors))  10.6 us
    dot_general x8, matrix products, one_query(): jnp.einsum('hqk,khd->qhd', weights.astype(jnp.bfloat16), value_flat, pref...  9.01 us
  transfers between devices with their start and end apart: 11, of which 9 were waited for; matrix products, arithmetic and copies ran while one was open for 48% of the time, Pallas kernels for 0%

profile of v1, /device:TPU:0, one launch (start us, length us, event | category | flops | bytes accessed | tf_op | source)
XLA Modules:
  0.0 302.0 jit_solution(14166030513742195780)
XLA Ops:
  6.5 4.6 %copy.34 = bf16[1,256,2048]{1,0,2:T(2,128)(2,1)S(1)} copy(bf16[1,256,2048]{2,1,0:T(8,128)(2,1)} %bitcast.104) | data formatting | bytes 2097152 | tf_op jit(solution)/shard_map/broadcast_in_dim | solution.py:32
  11.7 10.6 %reduce.3 = bf16[2048,256]{1,0:T(8,128)(2,1)S(1)} reduce(bf16[2048,1,256]{2,1,0:T(2,128)(2,1)S(1)} %bitcast.96, bf16[]{:T(256)} %broadcast.280), dimensions={1}, to_apply=%bitcast.49.reduce_sub_computation | reduce | bytes 2097154
  22.4 1.1 reshape.252
  23.5 7.3 %all-to-all-start.1 = ((bf16[8,2,32768]{2,1,0:T(2,128)(2,1)}), bf16[8,2,32768]{2,1,0:T(2,128)(2,1)S(1)}, u32[]{:S(2)}, u32[]{:S(2)}) async-start(bf16[8,2,32768]{2,1,0:T(2,128)(2,1)} %reshape.252), calls=%async_computation.1 | async-start | bytes 2097152 | tf_op jit(solution)/shard_map/all_to_all | solution.py:32
  30.8 4.6 %copy.36 = bf16[1,256,2048]{1,0,2:T(2,128)(2,1)S(1)} copy(bf16[1,256,2048]{2,1,0:T(8,128)(2,1)} %bitcast.105) | data formatting | bytes 2097152 | tf_op jit(solution)/shard_map/broadcast_in_dim | solution.py:33
  35.4 11.6 %reduce.4 = bf16[2048,256]{1,0:T(8,128)(2,1)} reduce(bf16[2048,1,256]{2,1,0:T(2,128)(2,1)S(1)} %bitcast.98, bf16[]{:T(256)} %broadcast.280), dimensions={1}, to_apply=%bitcast.51.reduce_sub_computation | reduce | bytes 2097154
  47.0 2.1 reshape.254
  49.2 7.4 %all-to-all-done.1 = bf16[8,2,32768]{2,1,0:T(2,128)(2,1)S(1)} async-done(((bf16[8,2,32768]{2,1,0:T(2,128)(2,1)}), bf16[8,2,32768]{2,1,0:T(2,128)(2,1)S(1)}, u32[]{:S(2)}, u32[]{:S(2)}) %all-to-all-start.1) | async-done | bytes 1048608 | tf_op jit(solution)/shard_map/all_to_all | solution.py:32
  56.5 4.3 %all-to-all-start.2 = ((bf16[8,2,32768]{2,1,0:T(2,128)(2,1)}), bf16[8,2,32768]{2,1,0:T(2,128)(2,1)}, u32[]{:S(2)}, u32[]{:S(2)}) async-start(bf16[8,2,32768]{2,1,0:T(2,128)(2,1)} %reshape.254), calls=%async_computation.2 | async-start | bytes 2097152 | tf_op jit(solution)/shard_map/all_to_all | solution.py:33
  60.8 4.6 %copy.33 = bf16[1,256,2048]{1,0,2:T(2,128)(2,1)S(1)} copy(bf16[1,256,2048]{2,1,0:T(8,128)(2,1)} %bitcast.106) | data formatting | bytes 2097152 | tf_op jit(solution)/shard_map/broadcast_in_dim | solution.py:31
  65.4 11.6 %reduce.2 = bf16[2048,256]{1,0:T(8,128)(2,1)} reduce(bf16[2048,1,256]{2,1,0:T(2,128)(2,1)S(1)} %bitcast.97, bf16[]{:T(256)} %broadcast.280), dimensions={1}, to_apply=%bitcast.47.reduce_sub_computation | reduce | bytes 2097154
  77.0 2.1 reshape.250
  79.1 7.2 %all-to-all-done.2 = bf16[8,2,32768]{2,1,0:T(2,128)(2,1)} async-done(((bf16[8,2,32768]{2,1,0:T(2,128)(2,1)}), bf16[8,2,32768]{2,1,0:T(2,128)(2,1)}, u32[]{:S(2)}, u32[]{:S(2)}) %all-to-all-start.2) | async-done | bytes 1048608 | tf_op jit(solution)/shard_map/all_to_all | solution.py:33
  86.4 4.3 %all-to-all-start = ((bf16[8,2,32768]{2,1,0:T(2,128)(2,1)}), bf16[8,2,32768]{2,1,0:T(2,128)(2,1)}, u32[]{:S(2)}, u32[]{:S(2)}) async-start(bf16[8,2,32768]{2,1,0:T(2,128)(2,1)} %reshape.250), calls=%async_computation | async-start | bytes 2097152 | tf_op jit(solution)/shard_map/all_to_all | solution.py:31
  90.7 1.9 collective-permute-start
  92.7 19.4 %collective-permute-done = s32[1,5]{1,0:T(1,128)S(1)} collective-permute-done((s32[1,5]{1,0:T(1,128)S(1)}, s32[1,5]{1,0:T(1,128)S(1)}, u32[]{:S(2)}, u32[]{:S(2)}) %collective-permute-start) | collective-permute-done | bytes 52 | tf_op jit(solution)/shard_map/ppermute | solution.py:40
  112.0 6.3 %collective-permute-done.1 = s32[1,5]{1,0:T(1,128)S(1)} collective-permute-done((s32[1,5]{1,0:T(1,128)S(1)}, s32[1,5]{1,0:T(1,128)S(1)}, u32[]{:S(2)}, u32[]{:S(2)}) %collective-permute-start.1) | collective-permute-done | bytes 52 | tf_op jit(solution)/shard_map/ppermute | solution.py:40
  118.3 6.3 %collective-permute-done.2 = s32[1,5]{1,0:T(1,128)S(1)} collective-permute-done((s32[1,5]{1,0:T(1,128)S(1)}, s32[1,5]{1,0:T(1,128)S(1)}, u32[]{:S(2)}, u32[]{:S(2)}) %collective-permute-start.2) | collective-permute-done | bytes 52 | tf_op jit(solution)/shard_map/ppermute | solution.py:40
  124.5 6.3 %collective-permute-done.3 = s32[1,5]{1,0:T(1,128)S(1)} collective-permute-done((s32[1,5]{1,0:T(1,128)S(1)}, s32[1,5]{1,0:T(1,128)S(1)}, u32[]{:S(2)}, u32[]{:S(2)}) %collective-permute-start.3) | collective-permute-done | bytes 52 | tf_op jit(solution)/shard_map/ppermute | solution.py:40
  130.8 6.3 %collective-permute-done.4 = s32[1,5]{1,0:T(1,128)S(1)} collective-permute-done((s32[1,5]{1,0:T(1,128)S(1)}, s32[1,5]{1,0:T(1,128)S(1)}, u32[]{:S(2)}, u32[]{:S(2)}) %collective-permute-start.4) | collective-permute-done | bytes 52 | tf_op jit(solution)/shard_map/ppermute | solution.py:40
  137.1 6.3 %collective-permute-done.5 = s32[1,5]{1,0:T(1,128)S(1)} collective-permute-done((s32[1,5]{1,0:T(1,128)S(1)}, s32[1,5]{1,0:T(1,128)S(1)}, u32[]{:S(2)}, u32[]{:S(2)}) %collective-permute-start.5) | collective-permute-done | bytes 52 | tf_op jit(solution)/shard_map/ppermute | solution.py:40
  143.3 6.3 %collective-permute-done.6 = s32[1,5]{1,0:T(1,128)S(1)} collective-permute-done((s32[1,5]{1,0:T(1,128)S(1)}, s32[1,5]{1,0:T(1,128)S(1)}, u32[]{:S(2)}, u32[]{:S(2)}) %collective-permute-start.6) | collective-permute-done | bytes 52 | tf_op jit(solution)/shard_map/ppermute | solution.py:40
  149.7 1.1 reshape.253
  152.7 4.3 %reshape.255 = bf16[2048,1,256]{2,1,0:T(2,128)(2,1)S(1)} reshape(bf16[8,2,32768]{2,1,0:T(2,128)(2,1)} %all-to-all-done.2) | data formatting | bytes 2097152
  157.9 1.4 reshape.233
  159.3 4.3 %reshape.251 = bf16[2048,1,256]{2,1,0:T(2,128)(2,1)S(1)} reshape(bf16[8,2,32768]{2,1,0:T(2,128)(2,1)} %all-to-all-done) | data formatting | bytes 2097152
  163.6 1.1 copy.40
  164.8 102.6 %while.18 = (s32[]{:T(128)}, bf16[8,256,256]{1,2,0:T(8,128)(2,1)}, s32[8]{0:T(128)S(1)}, s32[8,5]{1,0:T(8,128)S(1)}, s32[]{:T(128)}, /*index=5*/bf16[8,256,256]{...) while((s32[]{:T(128)}, bf16[8,256,256]{1,2,0:T(8,128)(2,1)}, ...), condition=%wide.region_4.5_spmd.clone, body=%wide.region_0.4_spmd.clone.sunk | while | flops 548549760 | bytes 19694732 | solution.py:70
  168.1 4.9 %select_select_fusion.2 = pred[2048]{0:T(1024)(128)(4,1)S(1)} fusion(pred[2048]{0:T(1024)(128)(4,1)S(1)} %get-tuple-element.493, pred[2048]{0:T(1024)(128)(4,1)S(1)} %get-tuple-element.494, pred[2048]{0:T(1024)(128)(4,1)S(1)} %get-tuple-element.495, pred[2048]{0:T(1024)(128)(4,1)S(1)} %get-tuple-element.496, ...), kind=kLoop, calls=%fused_computation.10.clone.1 | loop fusion | flops 14336 | bytes 16392 | tf_op jit(solution)/shard_map/while/body/eval_jaxpr/jit(_take)/gather | solution.py:51
  175.8 1.1 fusion.42
  180.9 4.9 %select_select_fusion.2 = pred[2048]{0:T(1024)(128)(4,1)S(1)} fusion(pred[2048]{0:T(1024)(128)(4,1)S(1)} %get-tuple-element.493, pred[2048]{0:T(1024)(128)(4,1)S(1)} %get-tuple-element.494, pred[2048]{0:T(1024)(128)(4,1)S(1)} %get-tuple-element.495, pred[2048]{0:T(1024)(128)(4,1)S(1)} %get-tuple-element.496, ...), kind=kLoop, calls=%fused_computation.10.clone.1 | loop fusion | flops 14336 | bytes 16392 | tf_op jit(solution)/shard_map/while/body/eval_jaxpr/jit(_take)/gather | solution.py:51
  187.7 0.9 fusion.41
  188.6 1.1 fusion.42
  193.7 4.9 %select_select_fusion.2 = pred[2048]{0:T(1024)(128)(4,1)S(1)} fusion(pred[2048]{0:T(1024)(128)(4,1)S(1)} %get-tuple-element.493, pred[2048]{0:T(1024)(128)(4,1)S(1)} %get-tuple-element.494, pred[2048]{0:T(1024)(128)(4,1)S(1)} %get-tuple-element.495, pred[2048]{0:T(1024)(128)(4,1)S(1)} %get-tuple-element.496, ...), kind=kLoop, calls=%fused_computation.10.clone.1 | loop fusion | flops 14336 | bytes 16392 | tf_op jit(solution)/shard_map/while/body/eval_jaxpr/jit(_take)/gather | solution.py:51
  200.5 0.9 fusion.41
  201.4 1.1 fusion.42
  206.5 4.9 %select_select_fusion.2 = pred[2048]{0:T(1024)(128)(4,1)S(1)} fusion(pred[2048]{0:T(1024)(128)(4,1)S(1)} %get-tuple-element.493, pred[2048]{0:T(1024)(128)(4,1)S(1)} %get-tuple-element.494, pred[2048]{0:T(1024)(128)(4,1)S(1)} %get-tuple-element.495, pred[2048]{0:T(1024)(128)(4,1)S(1)} %get-tuple-element.496, ...), kind=kLoop, calls=%fused_computation.10.clone.1 | loop fusion | flops 14336 | bytes 16392 | tf_op jit(solution)/shard_map/while/body/eval_jaxpr/jit(_take)/gather | solution.py:51
  214.3 1.1 fusion.42
  219.4 4.9 %select_select_fusion.2 = pred[2048]{0:T(1024)(128)(4,1)S(1)} fusion(pred[2048]{0:T(1024)(128)(4,1)S(1)} %get-tuple-element.493, pred[2048]{0:T(1024)(128)(4,1)S(1)} %get-tuple-element.494, pred[2048]{0:T(1024)(128)(4,1)S(1)} %get-tuple-element.495, pred[2048]{0:T(1024)(128)(4,1)S(1)} %get-tuple-element.496, ...), kind=kLoop, calls=%fused_computation.10.clone.1 | loop fusion | flops 14336 | bytes 16392 | tf_op jit(solution)/shard_map/while/body/eval_jaxpr/jit(_take)/gather | solution.py:51
  227.1 1.1 fusion.42
  232.2 4.9 %select_select_fusion.2 = pred[2048]{0:T(1024)(128)(4,1)S(1)} fusion(pred[2048]{0:T(1024)(128)(4,1)S(1)} %get-tuple-element.493, pred[2048]{0:T(1024)(128)(4,1)S(1)} %get-tuple-element.494, pred[2048]{0:T(1024)(128)(4,1)S(1)} %get-tuple-element.495, pred[2048]{0:T(1024)(128)(4,1)S(1)} %get-tuple-element.496, ...), kind=kLoop, calls=%fused_computation.10.clone.1 | loop fusion | flops 14336 | bytes 16392 | tf_op jit(solution)/shard_map/while/body/eval_jaxpr/jit(_take)/gather | solution.py:51
  239.9 1.1 fusion.42
  245.0 4.9 %select_select_fusion.2 = pred[2048]{0:T(1024)(128)(4,1)S(1)} fusion(pred[2048]{0:T(1024)(128)(4,1)S(1)} %get-tuple-element.493, pred[2048]{0:T(1024)(128)(4,1)S(1)} %get-tuple-element.494, pred[2048]{0:T(1024)(128)(4,1)S(1)} %get-tuple-element.495, pred[2048]{0:T(1024)(128)(4,1)S(1)} %get-tuple-element.496, ...), kind=kLoop, calls=%fused_computation.10.clone.1 | loop fusion | flops 14336 | bytes 16392 | tf_op jit(solution)/shard_map/while/body/eval_jaxpr/jit(_take)/gather | solution.py:51
  252.7 1.1 fusion.42
  257.8 4.9 %select_select_fusion.2 = pred[2048]{0:T(1024)(128)(4,1)S(1)} fusion(pred[2048]{0:T(1024)(128)(4,1)S(1)} %get-tuple-element.493, pred[2048]{0:T(1024)(128)(4,1)S(1)} %get-tuple-element.494, pred[2048]{0:T(1024)(128)(4,1)S(1)} %get-tuple-element.495, pred[2048]{0:T(1024)(128)(4,1)S(1)} %get-tuple-element.496, ...), kind=kLoop, calls=%fused_computation.10.clone.1 | loop fusion | flops 14336 | bytes 16392 | tf_op jit(solution)/shard_map/while/body/eval_jaxpr/jit(_take)/gather | solution.py:51
  265.6 1.1 fusion.42
  267.4 21.1 %all_to_all.63 = bf16[8,256,256]{1,2,0:T(8,128)(2,1)S(1)} all-to-all(bf16[8,256,256]{1,2,0:T(8,128)(2,1)} %get-tuple-element.287), channel_id=1, replica_groups=mesh['lat'=4,'lon'=8] {'lon'}, dimensions={0} | all-to-all | bytes 2097152 | tf_op jit(solution)/shard_map/all_to_all | solution.py:71
  288.5 6.7 %convolution_convert_fusion = bf16[256,2048]{1,0:T(8,128)(2,1)} fusion(bf16[256,2048]{0,1:T(8,128)(2,1)S(1)} %bitcast.99, bf16[2048,2048]{1,0:T(8,128)(2,1)} %all-gather.2.cloned.1.call-done), kind=kOutput, calls=%fused_computation.20 | convolution fusion | flops 2148007936 | bytes 10485760 | tf_op jit(solution)/shard_map/dot_general | solution.py:73
  (123 shorter events, 45.2 us)
Async XLA Ops:
  23.5 33.1 %all-to-all-start.1 = ((bf16[8,2,32768]{2,1,0:T(2,128)(2,1)}), bf16[8,2,32768]{2,1,0:T(2,128)(2,1)S(1)}, u32[]{:S(2)}, u32[]{:S(2)}) async-start(bf16[8,2,32768]{2,1,0:T(2,128)(2,1)} %reshape.252), calls=%async_computation.1 | async-start | bytes 2097152 | tf_op jit(solution)/shard_map/all_to_all | solution.py:32
  56.5 29.8 %all-to-all-start.2 = ((bf16[8,2,32768]{2,1,0:T(2,128)(2,1)}), bf16[8,2,32768]{2,1,0:T(2,128)(2,1)}, u32[]{:S(2)}, u32[]{:S(2)}) async-start(bf16[8,2,32768]{2,1,0:T(2,128)(2,1)} %reshape.254), calls=%async_computation.2 | async-start | bytes 2097152 | tf_op jit(solution)/shard_map/all_to_all | solution.py:33
  65.4 25.3 %copy-start.8 = (s32[1,5]{1,0:T(1,128)S(1)}, s32[1,5]{1,0:T(1,128)}, u32[]{:S(2)}) copy-start(s32[1,5]{1,0:T(1,128)} %param.12) | copy-start | bytes 64
  86.4 72.9 %all-to-all-start = ((bf16[8,2,32768]{2,1,0:T(2,128)(2,1)}), bf16[8,2,32768]{2,1,0:T(2,128)(2,1)}, u32[]{:S(2)}, u32[]{:S(2)}) async-start(bf16[8,2,32768]{2,1,0:T(2,128)(2,1)} %reshape.250), calls=%async_computation | async-start | bytes 2097152 | tf_op jit(solution)/shard_map/all_to_all | solution.py:31
  90.6 197.9 %all-gather.2.cloned.1.call-start = ((), (), s32[]{:S(2)}) async-start(), calls=%async_computation.4 | async-start | bytes 10485760 | tf_op jit(solution)/shard_map/all_gather | solution.py:75
  90.7 21.3 %collective-permute-start = (s32[1,5]{1,0:T(1,128)S(1)}, s32[1,5]{1,0:T(1,128)S(1)}, u32[]{:S(2)}, u32[]{:S(2)}) collective-permute-start(s32[1,5]{1,0:T(1,128)S(1)} %copy-done.8), channel_id=1, source_target_pairs={{0,1},{1,2},{2,3},{3,4},{4,5},{5,6},{6,7},{7,0},{8,9},{9,10},{10,1... | collective-permute-start | bytes 68 | tf_op jit(solution)/shard_map/ppermute | solution.py:40
  112.0 6.3 %collective-permute-start.1 = (s32[1,5]{1,0:T(1,128)S(1)}, s32[1,5]{1,0:T(1,128)S(1)}, u32[]{:S(2)}, u32[]{:S(2)}) collective-permute-start(s32[1,5]{1,0:T(1,128)S(1)} %collective-permute-done), channel_id=1, source_target_pairs={{0,1},{1,2},{2,3},{3,4},{4,5},{5,6},{6,7},{7,0},{8,9},{9,10},{10,1... | collective-permute-start | bytes 68 | tf_op jit(solution)/shard_map/ppermute | solution.py:40
  118.3 6.3 %collective-permute-start.2 = (s32[1,5]{1,0:T(1,128)S(1)}, s32[1,5]{1,0:T(1,128)S(1)}, u32[]{:S(2)}, u32[]{:S(2)}) collective-permute-start(s32[1,5]{1,0:T(1,128)S(1)} %collective-permute-done.1), channel_id=1, source_target_pairs={{0,1},{1,2},{2,3},{3,4},{4,5},{5,6},{6,7},{7,0},{8,9},{9,10},{10,1... | collective-permute-start | bytes 68 | tf_op jit(solution)/shard_map/ppermute | solution.py:40
  124.5 6.3 %collective-permute-start.3 = (s32[1,5]{1,0:T(1,128)S(1)}, s32[1,5]{1,0:T(1,128)S(1)}, u32[]{:S(2)}, u32[]{:S(2)}) collective-permute-start(s32[1,5]{1,0:T(1,128)S(1)} %collective-permute-done.2), channel_id=1, source_target_pairs={{0,1},{1,2},{2,3},{3,4},{4,5},{5,6},{6,7},{7,0},{8,9},{9,10},{10,1... | collective-permute-start | bytes 68 | tf_op jit(solution)/shard_map/ppermute | solution.py:40
  130.8 6.3 %collective-permute-start.4 = (s32[1,5]{1,0:T(1,128)S(1)}, s32[1,5]{1,0:T(1,128)S(1)}, u32[]{:S(2)}, u32[]{:S(2)}) collective-permute-start(s32[1,5]{1,0:T(1,128)S(1)} %collective-permute-done.3), channel_id=1, source_target_pairs={{0,1},{1,2},{2,3},{3,4},{4,5},{5,6},{6,7},{7,0},{8,9},{9,10},{10,1... | collective-permute-start | bytes 68 | tf_op jit(solution)/shard_map/ppermute | solution.py:40
  137.1 6.3 %collective-permute-start.5 = (s32[1,5]{1,0:T(1,128)S(1)}, s32[1,5]{1,0:T(1,128)S(1)}, u32[]{:S(2)}, u32[]{:S(2)}) collective-permute-start(s32[1,5]{1,0:T(1,128)S(1)} %collective-permute-done.4), channel_id=1, source_target_pairs={{0,1},{1,2},{2,3},{3,4},{4,5},{5,6},{6,7},{7,0},{8,9},{9,10},{10,1... | collective-permute-start | bytes 68 | tf_op jit(solution)/shard_map/ppermute | solution.py:40
  143.3 6.3 %collective-permute-start.6 = (s32[1,5]{1,0:T(1,128)S(1)}, s32[1,5]{1,0:T(1,128)S(1)}, u32[]{:S(2)}, u32[]{:S(2)}) collective-permute-start(s32[1,5]{1,0:T(1,128)S(1)} %collective-permute-done.5), channel_id=1, source_target_pairs={{0,1},{1,2},{2,3},{3,4},{4,5},{5,6},{6,7},{7,0},{8,9},{9,10},{10,1... | collective-permute-start | bytes 68 | tf_op jit(solution)/shard_map/ppermute | solution.py:40
  157.8 6.9 %copy-start.1 = (pred[2048]{0:T(1024)(128)(4,1)S(1)}, pred[2048]{0:T(1024)(128)(4,1)}, u32[]{:S(2)}) copy-start(pred[2048]{0:T(1024)(128)(4,1)} %constant.349) | copy-start | bytes 6148
  157.8 6.9 %copy-start.2 = (pred[2048]{0:T(1024)(128)(4,1)S(1)}, pred[2048]{0:T(1024)(128)(4,1)}, u32[]{:S(2)}) copy-start(pred[2048]{0:T(1024)(128)(4,1)} %constant.350) | copy-start | bytes 6148
  157.8 6.9 %copy-start.3 = (pred[2048]{0:T(1024)(128)(4,1)S(1)}, pred[2048]{0:T(1024)(128)(4,1)}, u32[]{:S(2)}) copy-start(pred[2048]{0:T(1024)(128)(4,1)} %constant.351) | copy-start | bytes 6148
  157.8 6.9 %copy-start.4 = (pred[2048]{0:T(1024)(128)(4,1)S(1)}, pred[2048]{0:T(1024)(128)(4,1)}, u32[]{:S(2)}) copy-start(pred[2048]{0:T(1024)(128)(4,1)} %constant.352) | copy-start | bytes 6148
  157.9 6.9 %copy-start.5 = (pred[2048]{0:T(1024)(128)(4,1)S(1)}, pred[2048]{0:T(1024)(128)(4,1)}, u32[]{:S(2)}) copy-start(pred[2048]{0:T(1024)(128)(4,1)} %constant.353) | copy-start | bytes 6148
  157.9 6.9 %copy-start.6 = (pred[2048]{0:T(1024)(128)(4,1)S(1)}, pred[2048]{0:T(1024)(128)(4,1)}, u32[]{:S(2)}) copy-start(pred[2048]{0:T(1024)(128)(4,1)} %constant.354) | copy-start | bytes 6148
  157.9 6.9 %copy-start.7 = (pred[2048]{0:T(1024)(128)(4,1)S(1)}, pred[2048]{0:T(1024)(128)(4,1)}, u32[]{:S(2)}) copy-start(pred[2048]{0:T(1024)(128)(4,1)} %constant.355) | copy-start | bytes 6148
  173.9 1.9 copy-start
  186.7 1.9 copy-start
  199.6 1.9 copy-start
  212.4 1.9 copy-start
  225.2 1.9 copy-start
  238.0 1.9 copy-start
  250.9 1.9 copy-start
  263.7 1.9 copy-start
Sparse Core Ops, SparseCore 0:
  93.0 59.5 all-gather.1
